TPU v7x, 32 devices: a whole 2x2x4 slice. The times are simulated.
32 devices in a mesh: vocab: 4 (over z), rows: 8 (over y, x, core).
Axes of the slice: x: 2, y: 2, z: 4, core: 2. Of those that a mesh axis runs over, the one named last changes fastest.
Arguments:
- trunk_hidden: bfloat16 [32, 7168], P('rows'), may hold values from -8 to 8
- mtp_state: bfloat16 [32, 7168], P('rows'), may hold values from -24 to 24, as said below
- mtp_gain: bfloat16 [7168], replicated, may hold values from 0.099609375 to 1.8984375
- head_weight: bfloat16 [4608, 7168], P(('vocab', 'rows')), may hold values from -0.28347335 to 0.28347335, as said below
- target_ids: int32 [32], replicated, may hold values from 0 to 4607
- mtp_target_ids: int32 [32], replicated, may hold values from 0 to 4607
- attn_values: bfloat16 [32, 16, 128], P('rows'), may hold values from -6 to 6
- out_proj: bfloat16 [2048, 7168], P('rows', 'vocab'), may hold values from -0.125 to 0.125
Outputs:
- grad_trunk: bfloat16 [32, 7168], P('rows')
- grad_residual: bfloat16 [32, 7168], P('rows')
- grad_gain: float32 [7168], replicated
- grad_head: bfloat16 [4608, 7168], P(('vocab', 'rows'))
- grad_attn: bfloat16 [32, 16, 128], P('vocab', 'rows')
- grad_out_proj: bfloat16 [2048, 7168], P('rows', 'vocab')
Inputs may be any that keep to these rules, and one draw needn't show every extreme that they name: `mtp_state`: block outputs; rows differ in scale. `head_weight`: head rows.
All inputs are finite; a program needn't handle non-finite values.
Results may differ from a plain program's by a relative error of at most 0.025.
Values may be sent and summed in bfloat16 or wider, within the bound.
No kernel may reach another device: no remote copies, remote signals or barrier semaphores. Data moves between devices by JAX's collectives and lax.ppermute only.
A program may use at most 64 MiB of HBM per device.

v0:
```python
import jax
import jax.numpy as jnp
from jax import lax
from jax.sharding import PartitionSpec as P

loss_scale = 8.0
mtp_share = 0.3
norm_eps = 1e-06


def merged(shard, axis, combine):
    everything = jax.tree.map(lambda part: lax.all_gather(part, axis), shard)
    initial = jax.tree.map(lambda part: part[0], everything)

    def lap(k, so_far):
        return combine(so_far, jax.tree.map(lambda part: part[k], everything))

    return lax.fori_loop(1, lax.axis_size(axis), lap, initial)


def normalize(state):
    values = state.astype(jnp.float32)
    inverse = lax.rsqrt(jnp.mean(values * values, axis=-1, keepdims=True) + norm_eps)
    return (values * inverse, inverse)


def local(
    trunk_hidden,
    mtp_state,
    mtp_gain,
    head_weight,
    target_ids,
    mtp_target_ids,
    attn_values,
    out_proj,
):
    tok_local = trunk_hidden.shape[0]
    row_count = lax.axis_size("rows")
    vocab_rows = head_weight.shape[0]
    gain = mtp_gain.astype(jnp.float32)
    normed, inverse = normalize(mtp_state)
    mtp_hidden = (normed * gain).astype(jnp.bfloat16)
    stacked = jnp.concatenate([trunk_hidden, mtp_hidden], axis=0)
    targets = jnp.stack(
        [target_ids.reshape(row_count, tok_local), mtp_target_ids.reshape(row_count, tok_local)],
        axis=1,
    ).reshape(-1)
    shares = jnp.stack(
        [
            jnp.full((row_count, tok_local), loss_scale, jnp.float32),
            jnp.full((row_count, tok_local), loss_scale * mtp_share, jnp.float32),
        ],
        axis=1,
    ).reshape(-1)
    block_index = lax.axis_index("vocab") * row_count + lax.axis_index("rows")
    vocab_ids = block_index * vocab_rows + jnp.arange(vocab_rows, dtype=jnp.int32)
    onehot = (targets[:, None] == vocab_ids[None, :]).astype(jnp.float32)
    gathered = lax.all_gather(stacked, "rows", axis=0, tiled=True)
    logits = lax.dot_general(
        gathered, head_weight, (((1,), (1,)), ((), ())), preferred_element_type=jnp.float32
    )
    local_max = jnp.max(logits, axis=1)
    local_total = jnp.sum(jnp.exp(logits - local_max[:, None]), axis=1)

    def combine(first, second):
        upper = jnp.maximum(first[0], second[0])
        return (
            upper,
            first[1] * jnp.exp(first[0] - upper) + second[1] * jnp.exp(second[0] - upper),
        )

    top, total = merged((local_max, local_total), ("vocab", "rows"), combine)
    logit_grads = (
        shares[:, None] * (jnp.exp(logits - top[:, None]) / total[:, None] - onehot)
    ).astype(jnp.bfloat16)
    feature_width = out_proj.shape[1]
    column_start = lax.axis_index("vocab") * feature_width
    own_terms = lax.psum_scatter(
        jnp.dot(logit_grads, head_weight, preferred_element_type=jnp.float32).astype(jnp.bfloat16),
        "rows",
        scatter_dimension=0,
        tiled=True,
    )
    grad_hidden = lax.psum(own_terms, "vocab").astype(jnp.float32)
    head_total = lax.dot_general(
        logit_grads, gathered, (((0,), (0,)), ((), ())), preferred_element_type=jnp.float32
    )
    grad_head = head_total.astype(jnp.bfloat16)
    grad_trunk = grad_hidden[:tok_local].astype(jnp.bfloat16)
    mtp_grad = grad_hidden[tok_local:]
    grad_gain = lax.psum(jnp.sum(mtp_grad * normed, axis=0), "rows")
    scaled = mtp_grad * gain
    dot_mean = jnp.mean(scaled * normed, axis=-1, keepdims=True)
    grad_residual = (inverse * (scaled - normed * dot_mean)).astype(jnp.bfloat16)
    own_columns = lax.dynamic_slice_in_dim(grad_residual, column_start, feature_width, 1)
    all_columns = lax.all_gather(own_columns, "rows", axis=0, tiled=True)
    partial_attn = lax.dot_general(
        all_columns, out_proj, (((1,), (1,)), ((), ())), preferred_element_type=jnp.float32
    )
    attn_share = lax.psum_scatter(
        partial_attn.astype(jnp.bfloat16), "vocab", scatter_dimension=0, tiled=True
    ).astype(jnp.float32)
    head_count = out_proj.shape[0] // attn_values.shape[2]
    grad_attn = attn_share.astype(jnp.bfloat16).reshape(
        attn_share.shape[0], head_count, attn_values.shape[2]
    )
    proj_grads = jnp.einsum(
        "tkh,td->khd",
        lax.all_to_all(attn_values, "rows", split_axis=1, concat_axis=0, tiled=True),
        all_columns,
        preferred_element_type=jnp.float32,
    ).astype(jnp.bfloat16)
    grad_out_proj = proj_grads.reshape(out_proj.shape[0], feature_width)
    return (grad_trunk, grad_residual, grad_gain, grad_head, grad_attn, grad_out_proj)


def solution(mesh):
    return jax.shard_map(
        local,
        mesh=mesh,
        in_specs=(
            P("rows", None),
            P("rows", None),
            P(),
            P(("vocab", "rows"), None),
            P(),
            P(),
            P("rows", None, None),
            P("rows", "vocab"),
        ),
        out_specs=(
            P("rows", None),
            P("rows", None),
            P(),
            P(("vocab", "rows"), None),
            P("vocab", "rows", None),
            P("rows", "vocab"),
        ),
        check_vma=False,
    )
```

profile of v0, /device:TPU:0, one launch (start us, length us, event | category | flops | bytes accessed | tf_op | source)
XLA Modules:
  0.0 189.2 jit_solution(16870470758866702679)
XLA Ops:
  7.2 0.0 reduce-scatter.3.cloned.1.call-start
  7.2 0.9 convert_element_type.38
  8.1 1.0 fusion.10
  9.1 0.9 fusion.8
  10.0 0.9 pad_maximum_fusion
  10.9 12.2 %all_gather.18 = bf16[64,7168]{1,0:T(8,128)(2,1)S(1)} all-gather(bf16[8,7168]{1,0:T(8,128)(2,1)S(1)} %pad_maximum_fusion), channel_id=1, replica_groups=mesh['vocab'=4,'rows'=8] {'rows'}, dimensions={0}, use_global_device_ids=true | all-gather | bytes 1032192 | tf_op jit(solution)/shard_map/all_gather | solution.py:58
  23.1 0.9 fusion.12
  24.0 0.2 exponential_reduce_fusion
  24.2 0.3 dynamic-update-slice
  24.5 0.3 dynamic-update-slice.1
  24.8 39.6 %all-reduce.2 = (f32[2048]{0:T(1024)S(1)}, f32[2048]{0:T(1024)S(1)}) all-reduce(f32[2048]{0:T(1024)S(1)} %dynamic-update-slice, f32[2048]{0:T(1024)S(1)} %dynamic-update-slice.1), channel_id=2, replica_groups=mesh['vocab'=4,'rows'=8] {'vocab','rows'}, use_global_device_ids=true, to_apply=%add | all-reduce | flops 4096 | bytes 32768
  64.3 0.1 reshape.41
  64.4 0.1 reshape.42
  64.5 1.4 while.17
  65.9 0.1 stack_reshape.7
  66.0 0.1 stack_reshape.6
  66.1 0.1 eq.15
  66.2 1.4 convolution_convert_fusion.1
  67.7 0.6 copy.21
  68.3 4.5 %all-to-all-start = ((bf16[4,16,128]{2,0,1:T(4,128)(2,1)}), bf16[4,16,128]{2,0,1:T(4,128)(2,1)S(1)}, u32[]{:S(2)}, u32[]{:S(2)}) async-start(bf16[4,16,128]{2,0,1:T(4,128)(2,1)} %copy.21), calls=%async_computation.2 | async-start | bytes 32768 | tf_op jit(solution)/shard_map/all_to_all | solution.py:109
  72.8 31.1 %reduce-scatter.3.cloned.1.call-done = bf16[8,7168]{1,0:T(8,128)(2,1)} async-done(((bf16[64,7168]{1,0:T(8,128)(2,1)}), bf16[8,7168]{1,0:T(8,128)(2,1)}) %reduce-scatter.3.cloned.1.call-update) | async-done | bytes 114704 | tf_op jit(solution)/shard_map/reduce_scatter | solution.py:78
  104.0 0.0 reduce-scatter.5.cloned.1.call-start
  104.0 2.1 %convolution_convert_fusion = bf16[144,7168]{1,0:T(8,128)(2,1)} fusion(bf16[64,7168]{1,0:T(8,128)(2,1)S(1)} %all_gather.18, f32[64,144]{1,0:T(8,128)S(1)} %get-tuple-element.176, s32[144]{0:T(256)S(1)} %iota_add_fusion, f32[64]{0:T(128)S(1)} %get-tuple-element.140, f32[64]{0:T(128)S(1)} %get-tuple-element.139, f32[64]{0:T(128)S(1)} %copy-done.5, s32[64]{0:T(128)S(1)} %eq.15), kind=kOutput, calls=%fused_computation.6 | convolution fusion | flops 133217280 | bytes 3020352 | tf_op jit(solution)/shard_map/dot_general | solution.py:85
  106.2 34.5 %all-reduce.5.cloned.1.call-done = bf16[8,7168]{1,0:T(8,128)(2,1)} async-done(((bf16[8,7168]{1,0:T(8,128)(2,1)}), bf16[8,7168]{1,0:T(8,128)(2,1)}) %all-reduce.5.cloned.1.call-update) | async-done | bytes 114704 | tf_op jit(solution)/shard_map/psum | solution.py:84
  140.6 1.3 fusion.11
  141.9 1.0 fusion.7
  143.0 9.2 %all-gather.2 = bf16[8,4,1792]{2,1,0:T(4,128)(2,1)S(1)} all-gather(bf16[1,4,1792]{2,1,0:T(4,128)(2,1)S(1)} %dynamic-slice_bitcast_fusion), channel_id=1, replica_groups=mesh['vocab'=4,'rows'=8] {'rows'}, dimensions={0}, use_global_device_ids=true | all-gather | bytes 129024 | tf_op jit(solution)/shard_map/all_gather | solution.py:96
  152.3 2.2 %convolution_convert_fusion.3 = bf16[32,256]{1,0:T(8,128)(2,1)} fusion(bf16[32,1792]{1,0:T(8,128)(2,1)S(1)} %reshape.52, bf16[256,1792]{1,0:T(8,128)(2,1)} %param.17), kind=kOutput, calls=%fused_computation.9 | convolution fusion | flops 29368320 | bytes 1048576 | tf_op jit(solution)/shard_map/dot_general | solution.py:97
  154.5 1.4 convolution_convert_fusion.2
  155.9 0.6 slice.25
  156.5 24.9 %psum.15 = f32[7168]{0:T(1024)} all-reduce(f32[7168]{0:T(1024)S(1)} %get-tuple-element.159), channel_id=1, replica_groups=mesh['vocab'=4,'rows'=8] {'rows'}, use_global_device_ids=true, to_apply=%region_9.0 | all-reduce | flops 7168 | bytes 57344 | tf_op jit(solution)/shard_map/psum | solution.py:91
  181.4 1.3 copy.23
  (66 shorter events, 1.1 us)
Async XLA Ops:
  7.2 15.9 %copy-start = (bf16[144,7168]{1,0:T(8,128)(2,1)S(1)}, bf16[144,7168]{1,0:T(8,128)(2,1)}, u32[]{:S(2)}) copy-start(bf16[144,7168]{1,0:T(8,128)(2,1)} %param.13) | copy-start | bytes 6193156
  7.2 96.8 %reduce-scatter.3.cloned.1.call-start = ((), (), s32[]{:S(2)}) async-start(), calls=%async_computation.3 | async-start | bytes 1032192 | tf_op jit(solution)/shard_map/reduce_scatter | solution.py:78
  10.9 55.0 %copy-start.6 = (s32[32]{0:T(128)S(1)}, s32[32]{0:T(128)}, u32[]{:S(2)}) copy-start(s32[32]{0:T(128)} %param.15) | copy-start | bytes 388
  10.9 55.1 %copy-start.7 = (s32[32]{0:T(128)S(1)}, s32[32]{0:T(128)}, u32[]{:S(2)}) copy-start(s32[32]{0:T(128)} %param.14) | copy-start | bytes 388
  10.9 55.3 %copy-start.5 = (f32[64]{0:T(128)S(1)}, f32[64]{0:T(128)}, u32[]{:S(2)}) copy-start(f32[64]{0:T(128)} %constant.55.clone.1) | copy-start | bytes 772
  65.9 1.8 copy-start.4
  67.6 73.0 %copy-start.1 = (bf16[4,7168]{1,0:T(4,128)(2,1)S(1)}, bf16[4,7168]{1,0:T(4,128)(2,1)}, u32[]{:S(2)}) copy-start(bf16[4,7168]{1,0:T(4,128)(2,1)} %param.11) | copy-start | bytes 172036
  68.3 37.9 %all-to-all-start = ((bf16[4,16,128]{2,0,1:T(4,128)(2,1)}), bf16[4,16,128]{2,0,1:T(4,128)(2,1)S(1)}, u32[]{:S(2)}, u32[]{:S(2)}) async-start(bf16[4,16,128]{2,0,1:T(4,128)(2,1)} %copy.21), calls=%async_computation.2 | async-start | bytes 32768 | tf_op jit(solution)/shard_map/all_to_all | solution.py:109
  72.8 67.9 %all-reduce.5.cloned.1.call-start = ((), (), s32[]{:S(2)}) async-start(), calls=%async_computation.4 | async-start | bytes 229376 | tf_op jit(solution)/shard_map/psum | solution.py:84
  104.0 77.4 %reduce-scatter.5.cloned.1.call-start = ((), (), s32[]{:S(2)}) async-start(), calls=%async_computation.5 | async-start | bytes 20480 | tf_op jit(solution)/shard_map/reduce_scatter | solution.py:100
  140.6 15.2 %copy-start.2 = (bf16[8,7168]{1,0:T(8,128)(2,1)S(1)}, bf16[8,7168]{1,0:T(8,128)(2,1)}, u32[]{:S(2)}) copy-start(bf16[8,7168]{1,0:T(8,128)(2,1)} %all-reduce.5.cloned.1.call-done) | copy-start | bytes 344068
  142.9 39.7 %copy-start.3 = (bf16[4,7168]{1,0:T(4,128)(2,1)}, bf16[4,7168]{1,0:T(4,128)(2,1)S(1)}, u32[]{:S(2)}) copy-start(bf16[4,7168]{1,0:T(4,128)(2,1)S(1)} %fusion.7) | copy-start | bytes 172036
Sparse Core Ops, SparseCore 0:
  67.8 36.1 reduce-scatter.2
  106.3 34.3 all-reduce.4
  154.6 18.2 reduce-scatter.4
where the time goes:
time: 190 us; the launch traced here: 189 us
  blocking collectives  85.8 us (45%)
  waiting for transfers between devices  65.6 us (35%)
  between operations  13.9 us (7%)
  matrix products  8.03 us (4%)
  other arithmetic  7 us (4%)
  starting transfers between devices  4.63 us (2%)
  local copies, waits for them, and re-layouts  3.6 us (2%)
    unnamed x1, blocking collectives  39.6 us
    psum x1, waiting for transfers between devices, local(): grad_hidden = lax.psum(own_terms, 'vocab').astype(jnp.float32)  34.5 us
    reduce_scatter x1, waiting for transfers between devices, local(): lax.psum_scatter(jnp.dot(logit_grads, head_weight, preferred_element_type...  31.1 us
    psum x1, blocking collectives, local(): grad_gain = lax.psum(jnp.sum(mtp_grad * normed, axis=0), 'rows')  24.9 us
    all_gather x1, blocking collectives, local(): gathered = lax.all_gather(stacked, 'rows', axis=0, tiled=True)  12.2 us
    all_gather x1, blocking collectives, local(): all_columns = lax.all_gather(own_columns, 'rows', axis=0, tiled=True)  9.22 us
    all_to_all x1, starting transfers between devices, local(): lax.all_to_all(attn_values, 'rows', split_axis=1, concat_axis=0, tiled=True)  4.52 us
  transfers between devices with their start and end apart: 4, of which 2 were waited for; matrix products, arithmetic and copies ran while one was open for 3% of the time, Pallas kernels for 0%

commit v1 on v0

--- a/solution.py
+++ b/solution.py
@@ -88,7 +88,9 @@
     grad_head = head_total.astype(jnp.bfloat16)
     grad_trunk = grad_hidden[:tok_local].astype(jnp.bfloat16)
     mtp_grad = grad_hidden[tok_local:]
-    grad_gain = lax.psum(jnp.sum(mtp_grad * normed, axis=0), "rows")
+    part_2 = jnp.sum(mtp_grad * normed, axis=0)
+    parts = lax.all_gather(part_2, "rows")
+    grad_gain = jnp.sum(parts, axis=0)
     scaled = mtp_grad * gain
     dot_mean = jnp.mean(scaled * normed, axis=-1, keepdims=True)
     grad_residual = (inverse * (scaled - normed * dot_mean)).astype(jnp.bfloat16)

time: 190 us -> 181 us (0.953)
  blocking collectives: 85.8 us -> 70.2 us
  waiting for transfers between devices: 65.6 us -> 72.1 us
    psum x1 -> x0, blocking collectives: 24.9 us -> none  [local(): grad_gain = lax.psum(jnp.sum(mtp_grad * normed, axis=0), 'rows')]
    all_gather x0 -> x1, blocking collectives: none -> 9.23 us  [local(): parts = lax.all_gather(part_2, 'rows')]
    reduce_scatter x1, waiting for transfers between devices: 0.01 us -> 6.49 us  [local(): lax.psum_scatter(partial_attn.astype(jnp.bfloat16), 'vocab', scatter_dime...]
  transfers between devices with their start and end apart: 4 -> 4, of which waited for: 2 -> 3; matrix products, arithmetic and copies ran while one was open for 3% -> 3% of each run, Pallas kernels for 0% -> 0%
where the time goes in v1:
time: 181 us
  waiting for transfers between devices  72.1 us (40%)
  blocking collectives  70.2 us (39%)
  between operations  13.9 us (8%)
  matrix products  8.03 us (4%)
  other arithmetic  7.66 us (4%)
  starting transfers between devices  4.63 us (3%)
  local copies, waits for them, and re-layouts  3.64 us (2%)
    unnamed x1, blocking collectives  39.6 us
    psum x1, waiting for transfers between devices, local(): grad_hidden = lax.psum(own_terms, 'vocab').astype(jnp.float32)  34.5 us
    reduce_scatter x1, waiting for transfers between devices, local(): lax.psum_scatter(jnp.dot(logit_grads, head_weight, preferred_element_type...  31.1 us
    all_gather x1, blocking collectives, local(): gathered = lax.all_gather(stacked, 'rows', axis=0, tiled=True)  12.2 us
    all_gather x1, blocking collectives, local(): parts = lax.all_gather(part_2, 'rows')  9.23 us
    all_gather x1, blocking collectives, local(): all_columns = lax.all_gather(own_columns, 'rows', axis=0, tiled=True)  9.22 us
    reduce_scatter x1, waiting for transfers between devices, local(): lax.psum_scatter(partial_attn.astype(jnp.bfloat16), 'vocab', scatter_dime...  6.49 us
    all_to_all x1, starting transfers between devices, local(): lax.all_to_all(attn_values, 'rows', split_axis=1, concat_axis=0, tiled=True)  4.52 us
  transfers between devices with their start and end apart: 4, of which 3 were waited for; matrix products, arithmetic and copies ran while one was open for 3% of the time, Pallas kernels for 0%

profile of v1, /device:TPU:0, one launch (start us, length us, event | category | flops | bytes accessed | tf_op | source)
XLA Modules:
  0.0 180.7 jit_solution(9579891943069815210)
XLA Ops:
  7.2 0.9 convert_element_type.38
  8.1 1.0 fusion.10
  9.1 0.9 fusion.8
  10.0 0.9 pad_maximum_fusion
  10.9 12.2 %all_gather.24 = bf16[64,7168]{1,0:T(8,128)(2,1)S(1)} all-gather(bf16[8,7168]{1,0:T(8,128)(2,1)S(1)} %pad_maximum_fusion), channel_id=1, replica_groups=mesh['vocab'=4,'rows'=8] {'rows'}, dimensions={0}, use_global_device_ids=true | all-gather | bytes 1032192 | tf_op jit(solution)/shard_map/all_gather | solution.py:58
  23.1 0.9 fusion.12
  24.0 0.2 exponential_reduce_fusion
  24.2 0.3 dynamic-update-slice
  24.5 0.3 dynamic-update-slice.1
  24.8 39.6 %all-reduce.2 = (f32[2048]{0:T(1024)S(1)}, f32[2048]{0:T(1024)S(1)}) all-reduce(f32[2048]{0:T(1024)S(1)} %dynamic-update-slice, f32[2048]{0:T(1024)S(1)} %dynamic-update-slice.1), channel_id=2, replica_groups=mesh['vocab'=4,'rows'=8] {'vocab','rows'}, use_global_device_ids=true, to_apply=%add | all-reduce | flops 4096 | bytes 32768
  64.3 0.1 reshape.41
  64.4 0.1 reshape.42
  64.5 1.4 while.17
  65.9 0.1 stack_reshape.7
  66.0 0.1 stack_reshape.6
  66.1 0.1 eq.15
  66.2 1.4 convolution_convert_fusion.1
  67.6 0.6 copy.25
  68.3 4.5 %all-to-all-start = ((bf16[4,16,128]{2,0,1:T(4,128)(2,1)}), bf16[4,16,128]{2,0,1:T(4,128)(2,1)S(1)}, u32[]{:S(2)}, u32[]{:S(2)}) async-start(bf16[4,16,128]{2,0,1:T(4,128)(2,1)} %copy.25), calls=%async_computation.2 | async-start | bytes 32768 | tf_op jit(solution)/shard_map/all_to_all | solution.py:111
  72.8 31.1 %reduce-scatter.3.cloned.1.call-done = bf16[8,7168]{1,0:T(8,128)(2,1)} async-done(((bf16[64,7168]{1,0:T(8,128)(2,1)}), bf16[8,7168]{1,0:T(8,128)(2,1)}) %reduce-scatter.3.cloned.1.call-update) | async-done | bytes 114704 | tf_op jit(solution)/shard_map/reduce_scatter | solution.py:78
  104.0 2.1 %convolution_convert_fusion = bf16[144,7168]{1,0:T(8,128)(2,1)} fusion(bf16[64,7168]{1,0:T(8,128)(2,1)S(1)} %all_gather.24, f32[64,144]{1,0:T(8,128)S(1)} %get-tuple-element.182, s32[144]{0:T(256)S(1)} %iota_add_fusion, f32[64]{0:T(128)S(1)} %get-tuple-element.140, f32[64]{0:T(128)S(1)} %get-tuple-element.139, f32[64]{0:T(128)S(1)} %copy-done.5, s32[64]{0:T(128)S(1)} %eq.15), kind=kOutput, calls=%fused_computation.6 | convolution fusion | flops 133217280 | bytes 3020352 | tf_op jit(solution)/shard_map/dot_general | solution.py:85
  106.2 34.5 %all-reduce.5.cloned.1.call-done = bf16[8,7168]{1,0:T(8,128)(2,1)} async-done(((bf16[8,7168]{1,0:T(8,128)(2,1)}), bf16[8,7168]{1,0:T(8,128)(2,1)}) %all-reduce.5.cloned.1.call-update) | async-done | bytes 114704 | tf_op jit(solution)/shard_map/psum | solution.py:84
  140.6 1.3 fusion.11
  141.9 1.0 fusion.7
  143.0 9.2 %all-gather.3 = bf16[8,4,1792]{2,1,0:T(4,128)(2,1)S(1)} all-gather(bf16[1,4,1792]{2,1,0:T(4,128)(2,1)S(1)} %dynamic-slice_bitcast_fusion), channel_id=1, replica_groups=mesh['vocab'=4,'rows'=8] {'rows'}, dimensions={0}, use_global_device_ids=true | all-gather | bytes 129024 | tf_op jit(solution)/shard_map/all_gather | solution.py:98
  152.3 2.2 %convolution_convert_fusion.3 = bf16[32,256]{1,0:T(8,128)(2,1)} fusion(bf16[32,1792]{1,0:T(8,128)(2,1)S(1)} %reshape.53, bf16[256,1792]{1,0:T(8,128)(2,1)} %param.17), kind=kOutput, calls=%fused_computation.9 | convolution fusion | flops 29368320 | bytes 1048576 | tf_op jit(solution)/shard_map/dot_general | solution.py:99
  154.5 1.4 convolution_convert_fusion.2
  155.9 9.2 %all-gather.2 = f32[57344]{0:T(1024)S(1)} all-gather(f32[7168]{0:T(1024)S(1)} %get-tuple-element.165), channel_id=4, replica_groups=mesh['vocab'=4,'rows'=8] {'rows'}, dimensions={0}, use_global_device_ids=true | all-gather | bytes 258048 | tf_op jit(solution)/shard_map/all_gather | solution.py:92
  165.1 0.7 reduce_sum.49
  165.8 0.6 slice.25
  166.4 6.5 %reduce-scatter.5.cloned.1.call-done = bf16[8,256]{1,0:T(8,128)(2,1)} async-done(((bf16[32,256]{1,0:T(8,128)(2,1)}), bf16[8,256]{1,0:T(8,128)(2,1)}) %reduce-scatter.5.cloned.1.call-update) | async-done | bytes 4112 | tf_op jit(solution)/shard_map/reduce_scatter | solution.py:102
  172.9 1.3 copy.27
  (68 shorter events, 1.2 us)
Async XLA Ops:
  7.2 15.9 %copy-start = (bf16[144,7168]{1,0:T(8,128)(2,1)S(1)}, bf16[144,7168]{1,0:T(8,128)(2,1)}, u32[]{:S(2)}) copy-start(bf16[144,7168]{1,0:T(8,128)(2,1)} %param.13) | copy-start | bytes 6193156
  7.2 96.8 %reduce-scatter.3.cloned.1.call-start = ((), (), s32[]{:S(2)}) async-start(), calls=%async_computation.3 | async-start | bytes 1032192 | tf_op jit(solution)/shard_map/reduce_scatter | solution.py:78
  10.9 55.0 %copy-start.6 = (s32[32]{0:T(128)S(1)}, s32[32]{0:T(128)}, u32[]{:S(2)}) copy-start(s32[32]{0:T(128)} %param.15) | copy-start | bytes 388
  10.9 55.1 %copy-start.7 = (s32[32]{0:T(128)S(1)}, s32[32]{0:T(128)}, u32[]{:S(2)}) copy-start(s32[32]{0:T(128)} %param.14) | copy-start | bytes 388
  10.9 55.3 %copy-start.5 = (f32[64]{0:T(128)S(1)}, f32[64]{0:T(128)}, u32[]{:S(2)}) copy-start(f32[64]{0:T(128)} %constant.55.clone.1) | copy-start | bytes 772
  65.9 1.8 copy-start.4
  67.6 73.0 %copy-start.1 = (bf16[4,7168]{1,0:T(4,128)(2,1)S(1)}, bf16[4,7168]{1,0:T(4,128)(2,1)}, u32[]{:S(2)}) copy-start(bf16[4,7168]{1,0:T(4,128)(2,1)} %param.11) | copy-start | bytes 172036
  68.3 37.9 %all-to-all-start = ((bf16[4,16,128]{2,0,1:T(4,128)(2,1)}), bf16[4,16,128]{2,0,1:T(4,128)(2,1)S(1)}, u32[]{:S(2)}, u32[]{:S(2)}) async-start(bf16[4,16,128]{2,0,1:T(4,128)(2,1)} %copy.25), calls=%async_computation.2 | async-start | bytes 32768 | tf_op jit(solution)/shard_map/all_to_all | solution.py:111
  72.8 67.9 %all-reduce.5.cloned.1.call-start = ((), (), s32[]{:S(2)}) async-start(), calls=%async_computation.4 | async-start | bytes 229376 | tf_op jit(solution)/shard_map/psum | solution.py:84
  104.0 69.0 %reduce-scatter.5.cloned.1.call-start = ((), (), s32[]{:S(2)}) async-start(), calls=%async_computation.5 | async-start | bytes 20480 | tf_op jit(solution)/shard_map/reduce_scatter | solution.py:102
  140.6 25.2 %copy-start.2 = (bf16[8,7168]{1,0:T(8,128)(2,1)S(1)}, bf16[8,7168]{1,0:T(8,128)(2,1)}, u32[]{:S(2)}) copy-start(bf16[8,7168]{1,0:T(8,128)(2,1)} %all-reduce.5.cloned.1.call-done) | copy-start | bytes 344068
  142.9 31.3 %copy-start.3 = (bf16[4,7168]{1,0:T(4,128)(2,1)}, bf16[4,7168]{1,0:T(4,128)(2,1)S(1)}, u32[]{:S(2)}) copy-start(bf16[4,7168]{1,0:T(4,128)(2,1)S(1)} %fusion.7) | copy-start | bytes 172036
Sparse Core Ops, SparseCore 0:
  67.8 36.1 reduce-scatter.2
  106.3 34.3 all-reduce.4
  154.6 18.2 reduce-scatter.4
